TPU v7x, 256 devices: a whole 4x4x8 slice. The times are simulated.
256 devices in a mesh: frame: 16 (over z_hi, y, core), row: 16 (over x, z_lo).
Axes of the slice: x: 4, y: 4, z: 8 (z_hi: 2, z_lo: 4; z = z_hi * 4 + z_lo), core: 2. Of those that a mesh axis runs over, the one named last changes fastest.
Arguments:
- latent: bfloat16 [64, 32, 240, 320], P('frame', 'row'), may hold values from -6 to 6
- gain_one: float32 [320], replicated, may hold values from 0.1 to 1.9
- spatial_weight: bfloat16 [3, 3, 320, 320], replicated, may hold values from -0.109375 to 0.109375
- gain_two: float32 [320], replicated, may hold values from 0.1 to 1.9
- temporal_weight: bfloat16 [3, 320, 320], replicated, may hold values from -0.1875 to 0.1875
- gain_three: float32 [320], replicated, may hold values from 0.1 to 1.9
- query_weight: bfloat16 [320, 320], replicated, as said below
- key_weight: bfloat16 [320, 320], replicated, may hold values from -0.3125 to 0.3125
- value_weight: bfloat16 [320, 320], replicated, may hold values from -0.3125 to 0.3125
- out_weight: bfloat16 [320, 320], replicated, may hold values from -0.3125 to 0.3125
Outputs:
- block_out: float32 [64, 32, 240, 320], P('frame', 'row')
Inputs may be any that keep to these rules, and one draw needn't show every extreme that they name: `query_weight`: a projection matrix.
All inputs are finite; a program needn't handle non-finite values.
Results may differ from a plain program's by a relative error of at most 0.012.
The roundings to bfloat16 on the way count: a program that leaves them out, or rounds other values in their place, can miss the bound.
Values may be sent and summed in bfloat16 or wider, within the bound.
A program may use at most 128 MiB of HBM per device.

v0:
```python
import jax
import jax.numpy as jnp
from jax import lax
from jax.sharding import PartitionSpec as P

HEAD_DIM = 64


def extended(cells, sides, width):
    for axis, dim in sides:
        count = lax.axis_size(axis)
        ends = count - 1
        head = lax.slice_in_dim(cells, 0, width, axis=dim)
        tail = lax.slice_in_dim(cells, cells.shape[dim] - width, cells.shape[dim], axis=dim)
        cells = jnp.concatenate(
            [
                lax.ppermute(tail, axis, [(i, (i + 1) % count) for i in range(ends)]),
                cells,
                lax.ppermute(head, axis, [((i + 1) % count, i) for i in range(ends)]),
            ],
            axis=dim,
        )
    return cells


def rms_norm(values, gain):
    mean_sq = jnp.mean(values * values, axis=-1, keepdims=True)
    return values * lax.rsqrt(mean_sq + 1e-06) * gain


def project(normed, weight):
    chans = normed.shape[-1]
    flat = jnp.dot(normed.reshape(-1, chans), weight, preferred_element_type=jnp.float32)
    return flat.astype(jnp.bfloat16).reshape(normed.shape[:-1] + (weight.shape[1],))


def attend_heads(queries, keys, values):
    frames, pixels, chans = queries.shape
    heads = chans // HEAD_DIM
    q_split = queries.reshape(frames, pixels, heads, HEAD_DIM)
    k_split = keys.reshape(frames, pixels, heads, HEAD_DIM)
    v_split = values.reshape(frames, pixels, heads, HEAD_DIM)
    scores = jnp.einsum(
        "fphd,gphd->phfg", q_split, k_split, preferred_element_type=jnp.float32
    ) / jnp.sqrt(jnp.float32(HEAD_DIM))
    peak = jnp.max(scores, axis=-1, keepdims=True)
    expo = jnp.exp(scores - peak)
    total = jnp.sum(expo, axis=-1)
    weight = expo.astype(jnp.bfloat16)
    summed = jnp.einsum("phfg,gphd->fphd", weight, v_split, preferred_element_type=jnp.float32)
    summed = summed / jnp.transpose(total, (2, 0, 1))[..., None]
    return summed.reshape(frames, pixels, chans).astype(jnp.bfloat16)


def temporal_mix(padded, temporal_weight, frames):
    chans = padded.shape[-1]
    pixels = padded.shape[1]
    total = jnp.zeros((frames * pixels, chans), jnp.float32)
    for tap in range(3):
        total = total + jnp.dot(
            padded[tap : tap + frames].reshape(-1, chans),
            temporal_weight[tap],
            preferred_element_type=jnp.float32,
        )
    return total.reshape(frames, pixels, chans)


def local(
    latent,
    gain_one,
    spatial_weight,
    gain_two,
    temporal_weight,
    gain_three,
    query_weight,
    key_weight,
    value_weight,
    out_weight,
):
    frames_here, rows_here, width, chans = latent.shape
    source = latent.astype(jnp.float32)
    act_one = jax.nn.silu(rms_norm(source, gain_one)).astype(jnp.bfloat16)
    rimmed = extended(act_one, (("row", 1),), 1)
    spatial = lax.conv_general_dilated(
        rimmed,
        spatial_weight,
        (1, 1),
        ((0, 0), (1, 1)),
        dimension_numbers=("NHWC", "HWIO", "NHWC"),
        preferred_element_type=jnp.float32,
    )
    hidden_one = source + spatial
    pixels = rows_here * width
    hidden_flat = hidden_one.reshape(frames_here, pixels, chans)
    act_two = jax.nn.silu(rms_norm(hidden_flat, gain_two)).astype(jnp.bfloat16)
    padded = extended(act_two, (("frame", 0),), 1)
    temporal = temporal_mix(padded, temporal_weight, frames_here)
    hidden_two = hidden_flat + temporal
    normed = rms_norm(hidden_two, gain_three).astype(jnp.bfloat16)
    groups = lax.axis_size("frame")
    per_group = pixels // groups

    def attend_triple(triple):
        shape_in = triple[0].shape
        flat_q = triple[0].reshape(shape_in[0], shape_in[2], chans)
        flat_k = triple[1].reshape(shape_in[0], shape_in[2], chans)
        flat_v = triple[2].reshape(shape_in[0], shape_in[2], chans)
        return attend_heads(flat_q, flat_k, flat_v).reshape(shape_in)

    triple = (
        project(normed, query_weight).reshape(frames_here, groups, per_group, chans),
        project(normed, key_weight).reshape(frames_here, groups, per_group, chans),
        project(normed, value_weight).reshape(frames_here, groups, per_group, chans),
    )
    attended = attend_triple(
        (
            lax.all_to_all(triple[0], "frame", split_axis=1, concat_axis=0, tiled=True),
            lax.all_to_all(triple[1], "frame", split_axis=1, concat_axis=0, tiled=True),
            lax.all_to_all(triple[2], "frame", split_axis=1, concat_axis=0, tiled=True),
        )
    )
    returned = lax.all_to_all(attended, "frame", split_axis=0, concat_axis=1, tiled=True)
    mixed = jnp.dot(returned.reshape(-1, chans), out_weight, preferred_element_type=jnp.float32)
    result = hidden_two.reshape(-1, chans) + mixed
    return result.reshape(frames_here, rows_here, width, chans)


def solution(mesh):
    return jax.shard_map(
        local,
        mesh=mesh,
        in_specs=(P("frame", "row", None, None), P(), P(), P(), P(), P(), P(), P(), P(), P()),
        out_specs=P("frame", "row", None, None),
        check_vma=False,
    )
```

profile of v0, /device:TPU:39, one launch (start us, length us, event | category | flops | bytes accessed | tf_op | source)
XLA Modules:
  0.0 389.2 jit_solution(17123246703365757660)
XLA Ops:
  16.5 11.6 %collective-permute-done.1 = bf16[4,1,240,320]{2,3,1,0:T(8,128)(2,1)} collective-permute-done((bf16[4,1,240,320]{2,3,1,0:T(8,128)(2,1)}, bf16[4,1,240,320]{2,3,1,0:T(8,128)(2,1)}, u32[]{:S(2)}, u32[]{:S(2)}) %collective-permute-start.1) | collective-permute-done | bytes 614432 | tf_op jit(solution)/shard_map/ppermute | solution.py:19
  29.5 15.3 %collective-permute-done = bf16[4,1,240,320]{2,3,1,0:T(8,128)(2,1)} collective-permute-done((bf16[4,1,240,320]{2,3,1,0:T(8,128)(2,1)}, bf16[4,1,240,320]{2,3,1,0:T(8,128)(2,1)}, u32[]{:S(2)}, u32[]{:S(2)}) %collective-permute-start) | collective-permute-done | bytes 614432 | tf_op jit(solution)/shard_map/ppermute | solution.py:17
  52.1 5.8 %reshape.116 = bf16[4,4,8,31,320]{4,3,2,1,0:T(8,128)(2,1)} reshape(bf16[4,4,248,320]{3,2,1,0:T(8,128)(2,1)} %pad) | data formatting | bytes 5079040 | tf_op jit(solution)/shard_map/conv_general_dilated | solution.py:84
  61.6 6.6 %fusion.24 = f32[2,32,31,320]{3,1,2,0:T(8,128)S(1)} fusion(bf16[3,3,320,320]{3,2,1,0:T(8,128)(2,1)S(1)} %copy-done, bf16[4,4,8,33,320]{4,3,2,1,0:T(8,128)(2,1)S(1)} %fusion.4, pred[32,31]{0,1:T(8,128)(4,1)S(1)} %copy-done.16), kind=kOutput, calls=%fused_computation.43 | convolution fusion | flops 3657543680 | bytes 7087072 | tf_op jit(solution)/shard_map/conv_general_dilated | solution.py:84
  83.1 4.9 %copy.75 = bf16[4,2,240,320]{2,1,0,3:T(2,128)(2,1)} copy(bf16[4,2,240,320]{3,2,0,1:T(8,128)(2,1)} %multiply_convert_fusion) | data formatting | bytes 2457600 | tf_op jit(solution)/shard_map/convert_element_type | solution.py:95
  88.0 5.3 %convert_element_type.48 = bf16[1920,320]{0,1:T(8,128)(2,1)} reshape(bf16[4,2,240,320]{2,1,0,3:T(2,128)(2,1)} %copy.75) | data formatting | bytes 2457600 | tf_op jit(solution)/shard_map/convert_element_type | solution.py:95
  93.3 4.8 %reshape.108 = f32[4,480,320]{1,2,0:T(8,128)} reshape(f32[4,2,240,320]{2,1,3,0:T(2,128)} %copy.72) | data formatting | bytes 4915200 | tf_op jit(solution)/shard_map/reshape | solution.py:94
  109.4 5.1 %reshape.107 = f32[1920,320]{0,1:T(8,128)} reshape(f32[4,2,240,320]{2,1,0,3:T(2,128)} %copy.71) | data formatting | bytes 4915200 | tf_op jit(solution)/shard_map/reshape | solution.py:94
  130.0 4.0 %reshape.110 = bf16[1920,320]{0,1:T(8,128)(2,1)} reshape(bf16[4,480,320]{1,0,2:T(4,128)(2,1)} %copy.76) | data formatting | bytes 2457600 | tf_op jit(solution)/shard_map/reshape | solution.py:61
  140.4 6.7 %reshape.111 = f32[4,2,240,320]{2,1,0,3:T(2,128)} reshape(f32[1920,320]{0,1:T(8,128)} %convolution_add_fusion.1) | data formatting | bytes 4915200 | tf_op jit(solution)/shard_map/reshape | solution.py:65
  147.1 5.7 %copy.77 = f32[4,2,240,320]{3,2,0,1:T(8,128)} copy(f32[4,2,240,320]{2,1,0,3:T(2,128)} %reshape.111) | data formatting | bytes 4915200 | tf_op jit(solution)/shard_map/reshape | solution.py:65
  155.3 4.3 %multiply_convert_fusion.2 = (bf16[1920,320]{0,1:T(8,128)(2,1)S(1)}, f32[1920,320]{0,1:T(8,128)}) fusion(f32[320]{0:T(512)S(1)} %copy-done.15, f32[1920]{0:T(1024)S(1)} %rsqrt.35, f32[1920,320]{0,1:T(8,128)} %reshape.107, f32[1920,320]{0,1:T(8,128)} %convolution_add_fusion.1), kind=kLoop, calls=%fused_computation.42 | loop fusion | flops 2457600 | bytes 8610560 | tf_op jit(solution)/shard_map/convert_element_type | solution.py:99
  166.8 14.6 %all-to-all-start.2 = ((bf16[4,16,30,320]{3,0,2,1:T(4,128)(2,1)}), bf16[4,16,30,320]{3,0,2,1:T(4,128)(2,1)}, u32[]{:S(2)}, u32[]{:S(2)}) async-start(bf16[4,16,30,320]{3,0,2,1:T(4,128)(2,1)} %copy.86), calls=%async_computation.2 | async-start | bytes 2949120 | tf_op jit(solution)/shard_map/all_to_all | solution.py:118
  188.7 32.6 %all-to-all-done.2 = bf16[4,16,30,320]{3,0,2,1:T(4,128)(2,1)} async-done(((bf16[4,16,30,320]{3,0,2,1:T(4,128)(2,1)}), bf16[4,16,30,320]{3,0,2,1:T(4,128)(2,1)}, u32[]{:S(2)}, u32[]{:S(2)}) %all-to-all-start.2) | async-done | bytes 1228832 | tf_op jit(solution)/shard_map/all_to_all | solution.py:118
  221.3 5.0 %all-to-all-start.1 = ((bf16[4,16,30,320]{3,0,2,1:T(4,128)(2,1)}), bf16[4,16,30,320]{3,0,2,1:T(4,128)(2,1)S(1)}, u32[]{:S(2)}, u32[]{:S(2)}) async-start(bf16[4,16,30,320]{3,0,2,1:T(4,128)(2,1)} %copy.83), calls=%async_computation.1 | async-start | bytes 2949120 | tf_op jit(solution)/shard_map/all_to_all | solution.py:117
  235.7 27.8 %all-to-all-done.1 = bf16[4,16,30,320]{3,0,2,1:T(4,128)(2,1)S(1)} async-done(((bf16[4,16,30,320]{3,0,2,1:T(4,128)(2,1)}), bf16[4,16,30,320]{3,0,2,1:T(4,128)(2,1)S(1)}, u32[]{:S(2)}, u32[]{:S(2)}) %all-to-all-start.1) | async-done | bytes 1228832 | tf_op jit(solution)/shard_map/all_to_all | solution.py:117
  263.5 5.3 %all-to-all-start = ((bf16[4,16,30,320]{3,0,2,1:T(4,128)(2,1)}), bf16[4,16,30,320]{3,0,2,1:T(4,128)(2,1)S(1)}, u32[]{:S(2)}, u32[]{:S(2)}) async-start(bf16[4,16,30,320]{3,0,2,1:T(4,128)(2,1)} %copy.80), calls=%async_computation | async-start | bytes 2949120 | tf_op jit(solution)/shard_map/all_to_all | solution.py:119
  272.1 5.5 %reshape_reshape.23 = bf16[64,30,5,64]{3,2,0,1:T(8,128)(2,1)} reshape(bf16[16,4,1,30,320]{4,1,0,3,2:T(4,128)(2,1)} %copy.87) | data formatting | bytes 2457600 | tf_op jit(solution)/shard_map/reshape;reshape | solution.py:41
  279.6 5.5 %reshape_reshape.21 = bf16[64,30,5,64]{3,2,0,1:T(8,128)(2,1)} reshape(bf16[16,4,1,30,320]{4,1,0,3,2:T(4,128)(2,1)} %copy.84) | data formatting | bytes 2457600 | tf_op jit(solution)/shard_map/reshape;reshape | solution.py:40
  285.1 20.7 %all-to-all-done = bf16[4,16,30,320]{3,0,2,1:T(4,128)(2,1)S(1)} async-done(((bf16[4,16,30,320]{3,0,2,1:T(4,128)(2,1)}), bf16[4,16,30,320]{3,0,2,1:T(4,128)(2,1)S(1)}, u32[]{:S(2)}, u32[]{:S(2)}) %all-to-all-start) | async-done | bytes 1228832 | tf_op jit(solution)/shard_map/all_to_all | solution.py:119
  310.2 4.7 %multiply_reduce_fusion = (f32[30,5,64]{2,1,0:T(8,128)S(1)}, f32[30,5,64,64]{2,3,1,0:T(8,128)S(1)}) fusion(bf16[64,30,5,64]{3,2,0,1:T(8,128)(2,1)} %reshape_reshape.23, bf16[64,30,5,64]{3,2,0,1:T(8,128)(2,1)} %reshape_reshape.21), kind=kOutput, calls=%fused_computation.5 | convolution fusion | flops 79862400 | bytes 4953600 | tf_op jit(solution)/shard_map/fphd,gphd->phfg/dot_general | solution.py:43
  323.7 44.2 %all_to_all.60 = bf16[64,1,30,320]{3,2,1,0:T(8,128)(2,1)S(1)} all-to-all(bf16[64,1,30,320]{3,2,1,0:T(8,128)(2,1)S(1)} %copy.92), channel_id=1, replica_groups=mesh['frame'=16,'row'=16] {'frame'}, dimensions={0} | all-to-all | bytes 2457600 | tf_op jit(solution)/shard_map/all_to_all | solution.py:122
  378.0 6.9 %reshape.113 = f32[4,2,240,320]{2,1,0,3:T(2,128)} reshape(f32[1920,320]{0,1:T(8,128)} %convolution_add_fusion) | data formatting | bytes 4915200 | tf_op jit(solution)/shard_map/reshape | solution.py:125
  384.9 4.1 %copy.95 = f32[4,2,240,320]{2,3,1,0:T(8,128)} copy(f32[4,2,240,320]{2,1,0,3:T(2,128)} %reshape.113) | data formatting | bytes 4915200 | tf_op jit(solution)/shard_map/reshape | solution.py:125
  (98 shorter events, 131.5 us)
Async XLA Ops:
  0.0 61.6 %copy-start = (bf16[3,3,320,320]{3,2,1,0:T(8,128)(2,1)S(1)}, bf16[3,3,320,320]{3,2,1,0:T(8,128)(2,1)}, u32[]{:S(2)}) copy-start(bf16[3,3,320,320]{3,2,1,0:T(8,128)(2,1)} %param.12) | copy-start | bytes 5529604
  0.0 4.6 %copy-start.14 = (f32[320]{0:T(512)S(1)}, f32[320]{0:T(512)}, u32[]{:S(2)}) copy-start(f32[320]{0:T(512)} %param.11) | copy-start | bytes 3844
  2.7 1.9 copy-start.2
  5.5 1.1 copy-start.3
  9.9 18.2 %collective-permute-start.1 = (bf16[4,1,240,320]{2,3,1,0:T(8,128)(2,1)}, bf16[4,1,240,320]{2,3,1,0:T(8,128)(2,1)}, u32[]{:S(2)}, u32[]{:S(2)}) collective-permute-start(bf16[4,1,240,320]{2,3,1,0:T(8,128)(2,1)} %copy.66), channel_id=1, source_target_pairs={{1,0},{2,1},{3,2},{4,3},{5,4},{6,5},{7,6},{8,7},{9,8},{10,9},{11,1... | collective-permute-start | bytes 1843208 | tf_op jit(solution)/shard_map/ppermute | solution.py:19
  13.0 31.9 %collective-permute-start = (bf16[4,1,240,320]{2,3,1,0:T(8,128)(2,1)}, bf16[4,1,240,320]{2,3,1,0:T(8,128)(2,1)}, u32[]{:S(2)}, u32[]{:S(2)}) collective-permute-start(bf16[4,1,240,320]{2,3,1,0:T(8,128)(2,1)} %copy.65), channel_id=1, source_target_pairs={{0,1},{1,2},{2,3},{3,4},{4,5},{5,6},{6,7},{7,8},{8,9},{9,10},{10,1... | collective-permute-start | bytes 1843208 | tf_op jit(solution)/shard_map/ppermute | solution.py:17
  59.2 2.4 copy-start.16
  77.8 3.4 copy-start.13
  100.9 1.1 copy-start.5
  102.9 15.3 %collective-permute-start.3 = (bf16[1,480,320]{1,2,0:T(8,128)(2,1)}, bf16[1,480,320]{1,2,0:T(8,128)(2,1)S(1)}, u32[]{:S(2)}, u32[]{:S(2)}) collective-permute-start(bf16[1,480,320]{1,2,0:T(8,128)(2,1)} %get-tuple-element.13), channel_id=1, source_target_pairs={{16,0},{32,16},{48,32},{64,48},{80,64},{96,80},{112,96},{128,112},... | collective-permute-start | bytes 921608 | tf_op jit(solution)/shard_map/ppermute | solution.py:19
  106.3 11.9 %collective-permute-start.2 = (bf16[1,480,320]{1,2,0:T(8,128)(2,1)}, bf16[1,480,320]{1,2,0:T(8,128)(2,1)}, u32[]{:S(2)}, u32[]{:S(2)}) collective-permute-start(bf16[1,480,320]{1,2,0:T(8,128)(2,1)} %get-tuple-element.14), channel_id=1, source_target_pairs={{0,16},{16,32},{32,48},{48,64},{64,80},{80,96},{96,112},{112,128},... | collective-permute-start | bytes 921608 | tf_op jit(solution)/shard_map/ppermute | solution.py:17
  114.5 3.7 copy-start.6
  134.0 3.2 copy-start.7
  152.8 2.4 copy-start.15
  155.2 4.3 %copy-start.10 = (bf16[320,320]{1,0:T(8,128)(2,1)S(1)}, bf16[320,320]{1,0:T(8,128)(2,1)}, u32[]{:S(2)}) copy-start(bf16[320,320]{1,0:T(8,128)(2,1)} %param.17) | copy-start | bytes 614404
  164.6 16.9 %copy-start.11 = (bf16[320,320]{1,0:T(8,128)(2,1)S(1)}, bf16[320,320]{1,0:T(8,128)(2,1)}, u32[]{:S(2)}) copy-start(bf16[320,320]{1,0:T(8,128)(2,1)} %param.16) | copy-start | bytes 614404
  166.8 54.5 %all-to-all-start.2 = ((bf16[4,16,30,320]{3,0,2,1:T(4,128)(2,1)}), bf16[4,16,30,320]{3,0,2,1:T(4,128)(2,1)}, u32[]{:S(2)}, u32[]{:S(2)}) async-start(bf16[4,16,30,320]{3,0,2,1:T(4,128)(2,1)} %copy.86), calls=%async_computation.2 | async-start | bytes 2949120 | tf_op jit(solution)/shard_map/all_to_all | solution.py:118
  186.4 39.9 %copy-start.12 = (bf16[320,320]{1,0:T(8,128)(2,1)S(1)}, bf16[320,320]{1,0:T(8,128)(2,1)}, u32[]{:S(2)}) copy-start(bf16[320,320]{1,0:T(8,128)(2,1)} %param.18) | copy-start | bytes 614404
  221.3 42.2 %all-to-all-start.1 = ((bf16[4,16,30,320]{3,0,2,1:T(4,128)(2,1)}), bf16[4,16,30,320]{3,0,2,1:T(4,128)(2,1)S(1)}, u32[]{:S(2)}, u32[]{:S(2)}) async-start(bf16[4,16,30,320]{3,0,2,1:T(4,128)(2,1)} %copy.83), calls=%async_computation.1 | async-start | bytes 2949120 | tf_op jit(solution)/shard_map/all_to_all | solution.py:117
  263.5 42.3 %all-to-all-start = ((bf16[4,16,30,320]{3,0,2,1:T(4,128)(2,1)}), bf16[4,16,30,320]{3,0,2,1:T(4,128)(2,1)S(1)}, u32[]{:S(2)}, u32[]{:S(2)}) async-start(bf16[4,16,30,320]{3,0,2,1:T(4,128)(2,1)} %copy.80), calls=%async_computation | async-start | bytes 2949120 | tf_op jit(solution)/shard_map/all_to_all | solution.py:119
  314.9 2.1 copy-start.8
  368.7 5.6 %copy-start.4 = (f32[1920,320]{0,1:T(8,128)S(1)}, f32[1920,320]{0,1:T(8,128)}, u32[]{:S(2)}) copy-start(f32[1920,320]{0,1:T(8,128)} %get-tuple-element.6) | copy-start | bytes 7372804
  368.7 5.6 %copy-start.9 = (bf16[320,320]{1,0:T(8,128)(2,1)S(1)}, bf16[320,320]{1,0:T(8,128)(2,1)}, u32[]{:S(2)}) copy-start(bf16[320,320]{1,0:T(8,128)(2,1)} %param.19) | copy-start | bytes 614404
  378.0 10.9 %copy-start.1 = (bf16[3,3,320,320]{3,2,1,0:T(8,128)(2,1)S(1)}, bf16[3,3,320,320]{3,2,1,0:T(8,128)(2,1)}, u32[]{:S(2)}) copy-start(bf16[3,3,320,320]{3,2,1,0:T(8,128)(2,1)} %param.12) | copy-start | bytes 5529604
where the time goes:
time: 395 us; the launch traced here: 389 us
  local copies, waits for them, and re-layouts  143 us (36%)
  waiting for transfers between devices  108 us (27%)
  blocking collectives  44.2 us (11%)
  starting transfers between devices  36.9 us (9%)
  matrix products  31.5 us (8%)
  other arithmetic  25 us (6%)
    all_to_all x1, blocking collectives, local(): lax.all_to_all(attended, 'frame', split_axis=0, concat_axis=1, tiled=True)  44.2 us
    all_to_all x1, waiting for transfers between devices, local(): lax.all_to_all(triple[1], 'frame', split_axis=1, concat_axis=0, tiled=True)  32.6 us
    all_to_all x1, waiting for transfers between devices, local(): lax.all_to_all(triple[0], 'frame', split_axis=1, concat_axis=0, tiled=True)  27.8 us
    all_to_all x1, waiting for transfers between devices, local(): lax.all_to_all(triple[2], 'frame', split_axis=1, concat_axis=0, tiled=True)  20.7 us
    ppermute x2, waiting for transfers between devices, extended(): lax.ppermute(tail, axis, [(i, (i + 1) % count) for i in range(ends)])  15.3 us
    all_to_all x1, starting transfers between devices, local(): lax.all_to_all(triple[1], 'frame', split_axis=1, concat_axis=0, tiled=True)  14.6 us
    reshape x2, local copies, waits for them, and re-layouts, temporal_mix(): return total.reshape(frames, pixels, chans)  12.4 us
    ppermute x2, waiting for transfers between devices, extended(): lax.ppermute(head, axis, [((i + 1) % count, i) for i in range(ends)])  11.6 us
  transfers between devices with their start and end apart: 7, of which 5 were waited for; matrix products, arithmetic and copies ran while one was open for 11% of the time, Pallas kernels for 0%

commit v1 on v0

--- a/solution.py
+++ b/solution.py
@@ -115,7 +115,12 @@
     attended = attend_triple(
         (
             lax.all_to_all(triple[0], "frame", split_axis=1, concat_axis=0, tiled=True),
-            lax.all_to_all(triple[1], "frame", split_axis=1, concat_axis=0, tiled=True),
+            jnp.concatenate(
+                lax.all_to_all(
+                    jnp.stack(jnp.split(triple[1], lax.axis_size("frame"), axis=1)), "frame", 0, 0
+                ),
+                axis=0,
+            ),
             lax.all_to_all(triple[2], "frame", split_axis=1, concat_axis=0, tiled=True),
         )
     )

time: 395 us -> 395 us (level)
  no operation moved by 1% of the time
where the time goes in v1:
time: 395 us; the launch traced here: 389 us
  local copies, waits for them, and re-layouts  143 us (36%)
  waiting for transfers between devices  108 us (27%)
  blocking collectives  44.2 us (11%)
  starting transfers between devices  36.9 us (9%)
  matrix products  31.6 us (8%)
  other arithmetic  25 us (6%)
    all_to_all x1, blocking collectives, local(): lax.all_to_all(attended, 'frame', split_axis=0, concat_axis=1, tiled=True)  44.2 us
    all_to_all x1, waiting for transfers between devices, local(): lax.all_to_all(jnp.stack(jnp.split(triple[1], lax.axis_size('frame'), axi...  32.6 us
    all_to_all x1, waiting for transfers between devices, local(): lax.all_to_all(triple[0], 'frame', split_axis=1, concat_axis=0, tiled=True)  27.8 us
    all_to_all x1, waiting for transfers between devices, local(): lax.all_to_all(triple[2], 'frame', split_axis=1, concat_axis=0, tiled=True)  20.7 us
    ppermute x2, waiting for transfers between devices, extended(): lax.ppermute(tail, axis, [(i, (i + 1) % count) for i in range(ends)])  15.3 us
    all_to_all x1, starting transfers between devices, local(): lax.all_to_all(jnp.stack(jnp.split(triple[1], lax.axis_size('frame'), axi...  14.6 us
    reshape x2, local copies, waits for them, and re-layouts, temporal_mix(): return total.reshape(frames, pixels, chans)  12.4 us
    ppermute x2, waiting for transfers between devices, extended(): lax.ppermute(head, axis, [((i + 1) % count, i) for i in range(ends)])  11.6 us
  transfers between devices with their start and end apart: 7, of which 5 were waited for; matrix products, arithmetic and copies ran while one was open for 11% of the time, Pallas kernels for 0%

profile of v1, /device:TPU:39, one launch (start us, length us, event | category | flops | bytes accessed | tf_op | source)
XLA Modules:
  0.0 389.2 jit_solution(7045659449236924321)
XLA Ops:
  16.5 11.6 %collective-permute-done.1 = bf16[4,1,240,320]{2,3,1,0:T(8,128)(2,1)} collective-permute-done((bf16[4,1,240,320]{2,3,1,0:T(8,128)(2,1)}, bf16[4,1,240,320]{2,3,1,0:T(8,128)(2,1)}, u32[]{:S(2)}, u32[]{:S(2)}) %collective-permute-start.1) | collective-permute-done | bytes 614432 | tf_op jit(solution)/shard_map/ppermute | solution.py:19
  29.5 15.3 %collective-permute-done = bf16[4,1,240,320]{2,3,1,0:T(8,128)(2,1)} collective-permute-done((bf16[4,1,240,320]{2,3,1,0:T(8,128)(2,1)}, bf16[4,1,240,320]{2,3,1,0:T(8,128)(2,1)}, u32[]{:S(2)}, u32[]{:S(2)}) %collective-permute-start) | collective-permute-done | bytes 614432 | tf_op jit(solution)/shard_map/ppermute | solution.py:17
  52.1 5.8 %reshape.115 = bf16[4,4,8,31,320]{4,3,2,1,0:T(8,128)(2,1)} reshape(bf16[4,4,248,320]{3,2,1,0:T(8,128)(2,1)} %pad) | data formatting | bytes 5079040 | tf_op jit(solution)/shard_map/conv_general_dilated | solution.py:84
  61.6 6.6 %fusion.24 = f32[2,32,31,320]{3,1,2,0:T(8,128)S(1)} fusion(bf16[3,3,320,320]{3,2,1,0:T(8,128)(2,1)S(1)} %copy-done, bf16[4,4,8,33,320]{4,3,2,1,0:T(8,128)(2,1)S(1)} %fusion.4, pred[32,31]{0,1:T(8,128)(4,1)S(1)} %copy-done.16), kind=kOutput, calls=%fused_computation.43 | convolution fusion | flops 3657543680 | bytes 7087072 | tf_op jit(solution)/shard_map/conv_general_dilated | solution.py:84
  83.1 4.9 %copy.122 = bf16[4,2,240,320]{2,1,0,3:T(2,128)(2,1)} copy(bf16[4,2,240,320]{3,2,0,1:T(8,128)(2,1)} %multiply_convert_fusion) | data formatting | bytes 2457600 | tf_op jit(solution)/shard_map/convert_element_type | solution.py:95
  88.0 5.3 %convert_element_type.48 = bf16[1920,320]{0,1:T(8,128)(2,1)} reshape(bf16[4,2,240,320]{2,1,0,3:T(2,128)(2,1)} %copy.122) | data formatting | bytes 2457600 | tf_op jit(solution)/shard_map/convert_element_type | solution.py:95
  93.3 4.8 %reshape.107 = f32[4,480,320]{1,2,0:T(8,128)} reshape(f32[4,2,240,320]{2,1,3,0:T(2,128)} %copy.119) | data formatting | bytes 4915200 | tf_op jit(solution)/shard_map/reshape | solution.py:94
  109.4 5.1 %reshape.106 = f32[1920,320]{0,1:T(8,128)} reshape(f32[4,2,240,320]{2,1,0,3:T(2,128)} %copy.118) | data formatting | bytes 4915200 | tf_op jit(solution)/shard_map/reshape | solution.py:94
  130.0 4.0 %reshape.109 = bf16[1920,320]{0,1:T(8,128)(2,1)} reshape(bf16[4,480,320]{1,0,2:T(4,128)(2,1)} %copy.123) | data formatting | bytes 2457600 | tf_op jit(solution)/shard_map/reshape | solution.py:61
  140.4 6.7 %reshape.110 = f32[4,2,240,320]{2,1,0,3:T(2,128)} reshape(f32[1920,320]{0,1:T(8,128)} %convolution_add_fusion.1) | data formatting | bytes 4915200 | tf_op jit(solution)/shard_map/reshape | solution.py:65
  147.1 5.7 %copy.124 = f32[4,2,240,320]{3,2,0,1:T(8,128)} copy(f32[4,2,240,320]{2,1,0,3:T(2,128)} %reshape.110) | data formatting | bytes 4915200 | tf_op jit(solution)/shard_map/reshape | solution.py:65
  155.3 4.3 %multiply_convert_fusion.2 = (bf16[1920,320]{0,1:T(8,128)(2,1)S(1)}, f32[1920,320]{0,1:T(8,128)}) fusion(f32[320]{0:T(512)S(1)} %copy-done.15, f32[1920]{0:T(1024)S(1)} %rsqrt.35, f32[1920,320]{0,1:T(8,128)} %reshape.106, f32[1920,320]{0,1:T(8,128)} %convolution_add_fusion.1), kind=kLoop, calls=%fused_computation.42 | loop fusion | flops 2457600 | bytes 8610560 | tf_op jit(solution)/shard_map/convert_element_type | solution.py:99
  166.9 14.6 %all-to-all-start.2 = ((bf16[16,4,1,30,320]{4,1,3,2,0:T(4,128)(2,1)}), bf16[16,4,1,30,320]{4,1,3,2,0:T(4,128)(2,1)}, u32[]{:S(2)}, u32[]{:S(2)}) async-start(bf16[16,4,1,30,320]{4,1,3,2,0:T(4,128)(2,1)} %copy.149), calls=%async_computation.2 | async-start | bytes 2949120 | tf_op jit(solution)/shard_map/all_to_all | solution.py:119
  188.7 32.6 %all-to-all-done.2 = bf16[16,4,1,30,320]{4,1,3,2,0:T(4,128)(2,1)} async-done(((bf16[16,4,1,30,320]{4,1,3,2,0:T(4,128)(2,1)}), bf16[16,4,1,30,320]{4,1,3,2,0:T(4,128)(2,1)}, u32[]{:S(2)}, u32[]{:S(2)}) %all-to-all-start.2) | async-done | bytes 1228832 | tf_op jit(solution)/shard_map/all_to_all | solution.py:119
  221.4 5.0 %all-to-all-start.1 = ((bf16[4,16,30,320]{3,0,2,1:T(4,128)(2,1)}), bf16[4,16,30,320]{3,0,2,1:T(4,128)(2,1)S(1)}, u32[]{:S(2)}, u32[]{:S(2)}) async-start(bf16[4,16,30,320]{3,0,2,1:T(4,128)(2,1)} %copy.130), calls=%async_computation.1 | async-start | bytes 2949120 | tf_op jit(solution)/shard_map/all_to_all | solution.py:117
  235.7 27.8 %all-to-all-done.1 = bf16[4,16,30,320]{3,0,2,1:T(4,128)(2,1)S(1)} async-done(((bf16[4,16,30,320]{3,0,2,1:T(4,128)(2,1)}), bf16[4,16,30,320]{3,0,2,1:T(4,128)(2,1)S(1)}, u32[]{:S(2)}, u32[]{:S(2)}) %all-to-all-start.1) | async-done | bytes 1228832 | tf_op jit(solution)/shard_map/all_to_all | solution.py:117
  263.5 5.3 %all-to-all-start = ((bf16[4,16,30,320]{3,0,2,1:T(4,128)(2,1)}), bf16[4,16,30,320]{3,0,2,1:T(4,128)(2,1)S(1)}, u32[]{:S(2)}, u32[]{:S(2)}) async-start(bf16[4,16,30,320]{3,0,2,1:T(4,128)(2,1)} %copy.127), calls=%async_computation | async-start | bytes 2949120 | tf_op jit(solution)/shard_map/all_to_all | solution.py:124
  272.1 5.5 %reshape_reshape_reshape.3 = bf16[64,30,5,64]{3,2,0,1:T(8,128)(2,1)} reshape(bf16[16,4,1,30,320]{4,1,0,3,2:T(4,128)(2,1)} %copy.150) | data formatting | bytes 2457600 | tf_op jit(solution)/shard_map/reshape;reshape;reshape | solution.py:41
  279.6 5.5 %reshape_reshape.18 = bf16[64,30,5,64]{3,2,0,1:T(8,128)(2,1)} reshape(bf16[16,4,1,30,320]{4,1,0,3,2:T(4,128)(2,1)} %copy.131) | data formatting | bytes 2457600 | tf_op jit(solution)/shard_map/reshape;reshape | solution.py:40
  285.1 20.7 %all-to-all-done = bf16[4,16,30,320]{3,0,2,1:T(4,128)(2,1)S(1)} async-done(((bf16[4,16,30,320]{3,0,2,1:T(4,128)(2,1)}), bf16[4,16,30,320]{3,0,2,1:T(4,128)(2,1)S(1)}, u32[]{:S(2)}, u32[]{:S(2)}) %all-to-all-start) | async-done | bytes 1228832 | tf_op jit(solution)/shard_map/all_to_all | solution.py:124
  310.2 4.7 %multiply_reduce_fusion = (f32[30,5,64]{2,1,0:T(8,128)S(1)}, f32[30,5,64,64]{2,3,1,0:T(8,128)S(1)}) fusion(bf16[64,30,5,64]{3,2,0,1:T(8,128)(2,1)} %reshape_reshape_reshape.3, bf16[64,30,5,64]{3,2,0,1:T(8,128)(2,1)} %reshape_reshape.18), kind=kOutput, calls=%fused_computation.5 | convolution fusion | flops 79862400 | bytes 4953600 | tf_op jit(solution)/shard_map/fphd,gphd->phfg/dot_general | solution.py:43
  323.7 44.2 %all_to_all.50 = bf16[64,1,30,320]{3,2,1,0:T(8,128)(2,1)S(1)} all-to-all(bf16[64,1,30,320]{3,2,1,0:T(8,128)(2,1)S(1)} %copy.155), channel_id=1, replica_groups=mesh['frame'=16,'row'=16] {'frame'}, dimensions={0} | all-to-all | bytes 2457600 | tf_op jit(solution)/shard_map/all_to_all | solution.py:127
  378.0 6.9 %reshape.112 = f32[4,2,240,320]{2,1,0,3:T(2,128)} reshape(f32[1920,320]{0,1:T(8,128)} %convolution_add_fusion) | data formatting | bytes 4915200 | tf_op jit(solution)/shard_map/reshape | solution.py:130
  384.9 4.1 %copy.158 = f32[4,2,240,320]{2,3,1,0:T(8,128)} copy(f32[4,2,240,320]{2,1,0,3:T(2,128)} %reshape.112) | data formatting | bytes 4915200 | tf_op jit(solution)/shard_map/reshape | solution.py:130
  (114 shorter events, 131.4 us)
Async XLA Ops:
  0.0 61.6 %copy-start = (bf16[3,3,320,320]{3,2,1,0:T(8,128)(2,1)S(1)}, bf16[3,3,320,320]{3,2,1,0:T(8,128)(2,1)}, u32[]{:S(2)}) copy-start(bf16[3,3,320,320]{3,2,1,0:T(8,128)(2,1)} %param.12) | copy-start | bytes 5529604
  0.0 4.6 %copy-start.14 = (f32[320]{0:T(512)S(1)}, f32[320]{0:T(512)}, u32[]{:S(2)}) copy-start(f32[320]{0:T(512)} %param.11) | copy-start | bytes 3844
  2.7 1.9 copy-start.2
  5.5 1.1 copy-start.3
  9.9 18.2 %collective-permute-start.1 = (bf16[4,1,240,320]{2,3,1,0:T(8,128)(2,1)}, bf16[4,1,240,320]{2,3,1,0:T(8,128)(2,1)}, u32[]{:S(2)}, u32[]{:S(2)}) collective-permute-start(bf16[4,1,240,320]{2,3,1,0:T(8,128)(2,1)} %copy.113), channel_id=1, source_target_pairs={{1,0},{2,1},{3,2},{4,3},{5,4},{6,5},{7,6},{8,7},{9,8},{10,9},{11,1... | collective-permute-start | bytes 1843208 | tf_op jit(solution)/shard_map/ppermute | solution.py:19
  13.0 31.9 %collective-permute-start = (bf16[4,1,240,320]{2,3,1,0:T(8,128)(2,1)}, bf16[4,1,240,320]{2,3,1,0:T(8,128)(2,1)}, u32[]{:S(2)}, u32[]{:S(2)}) collective-permute-start(bf16[4,1,240,320]{2,3,1,0:T(8,128)(2,1)} %copy.112), channel_id=1, source_target_pairs={{0,1},{1,2},{2,3},{3,4},{4,5},{5,6},{6,7},{7,8},{8,9},{9,10},{10,1... | collective-permute-start | bytes 1843208 | tf_op jit(solution)/shard_map/ppermute | solution.py:17
  59.2 2.4 copy-start.16
  77.8 3.4 copy-start.13
  100.9 1.1 copy-start.5
  102.9 15.3 %collective-permute-start.3 = (bf16[1,480,320]{1,2,0:T(8,128)(2,1)}, bf16[1,480,320]{1,2,0:T(8,128)(2,1)S(1)}, u32[]{:S(2)}, u32[]{:S(2)}) collective-permute-start(bf16[1,480,320]{1,2,0:T(8,128)(2,1)} %get-tuple-element.13), channel_id=1, source_target_pairs={{16,0},{32,16},{48,32},{64,48},{80,64},{96,80},{112,96},{128,112},... | collective-permute-start | bytes 921608 | tf_op jit(solution)/shard_map/ppermute | solution.py:19
  106.3 11.9 %collective-permute-start.2 = (bf16[1,480,320]{1,2,0:T(8,128)(2,1)}, bf16[1,480,320]{1,2,0:T(8,128)(2,1)}, u32[]{:S(2)}, u32[]{:S(2)}) collective-permute-start(bf16[1,480,320]{1,2,0:T(8,128)(2,1)} %get-tuple-element.14), channel_id=1, source_target_pairs={{0,16},{16,32},{32,48},{48,64},{64,80},{80,96},{96,112},{112,128},... | collective-permute-start | bytes 921608 | tf_op jit(solution)/shard_map/ppermute | solution.py:17
  114.5 3.7 copy-start.6
  134.0 3.2 copy-start.7
  152.8 2.4 copy-start.15
  155.2 4.3 %copy-start.10 = (bf16[320,320]{1,0:T(8,128)(2,1)S(1)}, bf16[320,320]{1,0:T(8,128)(2,1)}, u32[]{:S(2)}) copy-start(bf16[320,320]{1,0:T(8,128)(2,1)} %param.17) | copy-start | bytes 614404
  165.0 16.5 %copy-start.11 = (bf16[320,320]{1,0:T(8,128)(2,1)S(1)}, bf16[320,320]{1,0:T(8,128)(2,1)}, u32[]{:S(2)}) copy-start(bf16[320,320]{1,0:T(8,128)(2,1)} %param.16) | copy-start | bytes 614404
  166.9 54.5 %all-to-all-start.2 = ((bf16[16,4,1,30,320]{4,1,3,2,0:T(4,128)(2,1)}), bf16[16,4,1,30,320]{4,1,3,2,0:T(4,128)(2,1)}, u32[]{:S(2)}, u32[]{:S(2)}) async-start(bf16[16,4,1,30,320]{4,1,3,2,0:T(4,128)(2,1)} %copy.149), calls=%async_computation.2 | async-start | bytes 2949120 | tf_op jit(solution)/shard_map/all_to_all | solution.py:119
  186.5 39.9 %copy-start.12 = (bf16[320,320]{1,0:T(8,128)(2,1)S(1)}, bf16[320,320]{1,0:T(8,128)(2,1)}, u32[]{:S(2)}) copy-start(bf16[320,320]{1,0:T(8,128)(2,1)} %param.18) | copy-start | bytes 614404
  221.4 42.2 %all-to-all-start.1 = ((bf16[4,16,30,320]{3,0,2,1:T(4,128)(2,1)}), bf16[4,16,30,320]{3,0,2,1:T(4,128)(2,1)S(1)}, u32[]{:S(2)}, u32[]{:S(2)}) async-start(bf16[4,16,30,320]{3,0,2,1:T(4,128)(2,1)} %copy.130), calls=%async_computation.1 | async-start | bytes 2949120 | tf_op jit(solution)/shard_map/all_to_all | solution.py:117
  263.5 42.3 %all-to-all-start = ((bf16[4,16,30,320]{3,0,2,1:T(4,128)(2,1)}), bf16[4,16,30,320]{3,0,2,1:T(4,128)(2,1)S(1)}, u32[]{:S(2)}, u32[]{:S(2)}) async-start(bf16[4,16,30,320]{3,0,2,1:T(4,128)(2,1)} %copy.127), calls=%async_computation | async-start | bytes 2949120 | tf_op jit(solution)/shard_map/all_to_all | solution.py:124
  315.0 2.1 copy-start.8
  368.7 5.6 %copy-start.4 = (f32[1920,320]{0,1:T(8,128)S(1)}, f32[1920,320]{0,1:T(8,128)}, u32[]{:S(2)}) copy-start(f32[1920,320]{0,1:T(8,128)} %get-tuple-element.6) | copy-start | bytes 7372804
  368.7 5.6 %copy-start.9 = (bf16[320,320]{1,0:T(8,128)(2,1)S(1)}, bf16[320,320]{1,0:T(8,128)(2,1)}, u32[]{:S(2)}) copy-start(bf16[320,320]{1,0:T(8,128)(2,1)} %param.19) | copy-start | bytes 614404
  378.0 10.9 %copy-start.1 = (bf16[3,3,320,320]{3,2,1,0:T(8,128)(2,1)S(1)}, bf16[3,3,320,320]{3,2,1,0:T(8,128)(2,1)}, u32[]{:S(2)}) copy-start(bf16[3,3,320,320]{3,2,1,0:T(8,128)(2,1)} %param.12) | copy-start | bytes 5529604
